TPU v7x, 256 devices: a whole 4x4x8 slice. The times are simulated.
256 devices in a mesh: section: 4 (over x), dp: 8 (over y, core), expert: 8 (over z).
Axes of the slice: x: 4, y: 4, z: 8, core: 2. Of those that a mesh axis runs over, the one named last changes fastest.
Arguments:
- patches: bfloat16 [32768, 1152], P(('dp', 'expert')), may hold values from -50 to 50
- lengths: int32 [64, 4], P(('dp', 'expert')), may hold values from 1 to 64, 128 in all within a row
- w_qkv: bfloat16 [1152, 3456], P(None, 'section'), may hold values from -4.714045 to 4.714045
- w_out: bfloat16 [1152, 1152], P('section'), may hold values from -0.1875 to 0.1875
- w_proj: bfloat16 [4608, 2048], P('dp', 'section'), may hold values from -0.09375 to 0.09375
- routes: int32 [8192, 6], P(('dp', 'expert')), may hold values from 0 to 63, all different within a row; in each aligned block of 128 rows (0 to 127, 128 to 255, ...) at most 24 rows name the same one
- gates: float32 [8192, 6], P(('dp', 'expert')), may hold values from 0.05 to 0.4
- w_gate: bfloat16 [64, 2048, 1408], P(('dp', 'expert'), None, 'section'), may hold values from -0.125 to 0.125
- w_up: bfloat16 [64, 2048, 1408], P(('dp', 'expert'), None, 'section'), may hold values from -0.125 to 0.125
- w_down: bfloat16 [64, 1408, 2048], P(('dp', 'expert'), 'section'), may hold values from -0.15625 to 0.15625
Outputs:
- language_out: bfloat16 [8192, 2048], P(('dp', 'expert'), 'section')
Inputs may be any that keep to these rules, and one draw needn't show every extreme that they name: Each row lists, in order, the lengths in merged tokens of a group's images; they sum to 128 and the largest is exactly 64. `routes`: A token's 6 experts differ. Among the rows of one device no expert is named more than 24 times, a bound that some block reaches in every draw.
All inputs are finite; a program needn't handle non-finite values.
Results may differ from a plain program's by a relative error of at most 0.012.
Values may be sent and summed in bfloat16 or wider, within the bound.
No kernel may reach another device: no remote copies, remote signals or barrier semaphores. Data moves between devices by JAX's collectives and lax.ppermute only.
A program may use at most 64 MiB of HBM per device.

v0:
```python
import math
import jax
import jax.numpy as jnp
from jax import lax
from jax.sharding import PartitionSpec as P

D_VIT = 1152
HEADS = 16
TOP = 6


def layer_norm(values):
    center = values - jnp.mean(values, axis=-1, keepdims=True)
    spread = jnp.mean(center * center, axis=-1, keepdims=True)
    return center * lax.rsqrt(spread + 1e-06)


def rms_norm(values):
    return values * lax.rsqrt(jnp.mean(values * values, axis=-1, keepdims=True) + 1e-06)


def per_device(patches, lengths, w_qkv, w_out, w_proj, routes, gates, w_gate, w_up, w_down):
    data_count = lax.axis_size("dp")
    owner_count = lax.axis_size("expert")
    patch_rows, width = patches.shape
    head_dim = D_VIT // HEADS
    local_heads = w_qkv.shape[1] // (3 * head_dim)
    scale = 1.0 / math.sqrt(head_dim)
    normed_in = layer_norm(patches.astype(jnp.float32)).astype(jnp.bfloat16)
    packed = jnp.dot(normed_in, w_qkv, preferred_element_type=jnp.float32).astype(jnp.bfloat16)
    packed = packed.reshape(patch_rows, local_heads, 3, head_dim)
    query = packed[:, :, 0]
    key_part = packed[:, :, 1]
    value_part = packed[:, :, 2]
    ends = jnp.cumsum(lengths[0]) * 4
    places = jnp.arange(patch_rows, dtype=jnp.int32)
    segment = jnp.sum((places[:, None] >= ends[None, :]).astype(jnp.int32), axis=1)
    block_rows = min(patch_rows, 512)
    block_count = patch_rows // block_rows

    def attend(blocks):
        query_block, segment_block = blocks
        scores = (
            jnp.einsum("qhd,khd->hqk", query_block, key_part, preferred_element_type=jnp.float32)
            * scale
        )
        same = segment_block[:, None] == segment[None, :]
        scores = jnp.where(same[None], scores, -jnp.inf)
        peak = jnp.max(scores, axis=-1, keepdims=True)
        weights = jnp.where(same[None], jnp.exp(scores - peak), 0.0)
        probs = (weights / jnp.sum(weights, axis=-1, keepdims=True)).astype(jnp.bfloat16)
        result = jnp.einsum("hqk,khd->qhd", probs, value_part, preferred_element_type=jnp.float32)
        return result.astype(jnp.bfloat16).reshape(block_rows, local_heads * head_dim)

    attended = lax.map(
        attend,
        (
            query.reshape(block_count, block_rows, local_heads, head_dim),
            segment.reshape(block_count, block_rows),
        ),
    )
    attended = attended.reshape(patch_rows, local_heads * head_dim)
    merged_count = patch_rows // 4
    summed = lax.psum(
        jnp.dot(attended, w_out, preferred_element_type=jnp.float32).astype(jnp.bfloat16), "section"
    ).astype(jnp.float32)
    merged = (
        (patches.astype(jnp.float32) + summed).reshape(merged_count, 4 * width).astype(jnp.bfloat16)
    )
    proj_own = jnp.dot(
        merged, lax.all_gather(w_proj, "dp", axis=0, tiled=True), preferred_element_type=jnp.float32
    ).astype(jnp.bfloat16)
    projected = lax.all_gather(proj_own, "section", axis=1, tiled=True)
    model_width = projected.shape[1]
    normed_tokens = rms_norm(projected.astype(jnp.float32)).astype(jnp.bfloat16)
    expert_total = data_count * owner_count
    capacity = max(2, min(merged_count, 2 * merged_count * TOP // expert_total))
    route_flat = routes.reshape(-1)
    onehot = (route_flat[:, None] == jnp.arange(expert_total, dtype=jnp.int32)[None, :]).astype(
        jnp.int32
    )
    ranks = jnp.cumsum(onehot, axis=0) - 1
    slots = jnp.sum(ranks * onehot, axis=1)
    target = route_flat * capacity + slots
    owners = jnp.arange(merged_count * TOP, dtype=jnp.int32) // TOP
    source = jnp.zeros((expert_total * capacity,), dtype=jnp.int32).at[target].set(owners)
    outgoing = normed_tokens[source].reshape(expert_total, capacity, model_width)
    received = lax.all_to_all(outgoing, ("dp", "expert"), split_axis=0, concat_axis=0, tiled=True)
    flat_rows = received.reshape(-1, received.shape[-1])
    gate_act = jnp.dot(flat_rows, w_gate[0], preferred_element_type=jnp.float32)
    up_act = jnp.dot(flat_rows, w_up[0], preferred_element_type=jnp.float32)
    hidden = (jax.nn.silu(gate_act) * up_act).astype(jnp.bfloat16)
    result = jnp.dot(hidden, w_down[0], preferred_element_type=jnp.float32).astype(jnp.bfloat16)
    returned = lax.all_to_all(
        result.reshape(received.shape[:-1] + (w_down.shape[2],)),
        ("dp", "expert"),
        split_axis=0,
        concat_axis=0,
        tiled=True,
    )
    picked = returned.reshape(expert_total * capacity, model_width)[target].reshape(
        merged_count, TOP, model_width
    )
    weighted = jnp.zeros((merged_count, model_width), dtype=jnp.float32)
    for choice_index in range(TOP):
        weighted = weighted + gates[:, choice_index : choice_index + 1] * picked[
            :, choice_index
        ].astype(jnp.float32)
    expert_cols = lax.psum_scatter(
        weighted.astype(jnp.bfloat16), "section", scatter_dimension=1, tiled=True
    ).astype(jnp.float32)
    return (proj_own.astype(jnp.float32) + expert_cols).astype(jnp.bfloat16)


def solution(mesh):
    return jax.shard_map(
        per_device,
        mesh=mesh,
        in_specs=(
            P(("dp", "expert"), None),
            P(("dp", "expert"), None),
            P(None, "section"),
            P("section", None),
            P("dp", "section"),
            P(("dp", "expert"), None),
            P(("dp", "expert"), None),
            P(("dp", "expert"), None, "section"),
            P(("dp", "expert"), None, "section"),
            P(("dp", "expert"), "section", None),
        ),
        out_specs=P(("dp", "expert"), "section"),
        check_vma=False,
    )
```

profile of v0, /device:TPU:8, one launch (start us, length us, event | category | flops | bytes accessed | tf_op | source)
XLA Modules:
  0.0 488.4 jit_solution(8950288940394244735)
XLA Ops:
  7.4 1.6 convert_reduce_fusion
  9.0 1.7 fusion.5
  11.3 2.4 convolution_convert_fusion.2
  13.7 4.9 %fusion.46 = (f32[4,512]{1,0:T(4,128)S(1)}, f32[4,512,512]{1,2,0:T(8,128)}) fusion(pred[512,512]{0,1:T(8,128)(4,1)S(1)} %broadcast_compare_fusion, bf16[512,4,3,72]{0,3,2,1:T(8,128)(2,1)} %bitcast.124), kind=kOutput, calls=%fused_computation.101 | convolution fusion | flops 156238336 | bytes 5316608 | tf_op jit(solution)/shard_map/while/body/eval_jaxpr/sub | solution.py:50
  18.7 2.8 fusion.16
  21.5 1.9 convolution_convert_fusion.1
  24.5 1.8 reduce-window.19
  27.0 3.4 scatter_custom_fusion
  30.4 47.7 %all-reduce.2.cloned.1.call-done = bf16[512,1152]{1,0:T(8,128)(2,1)} async-done(((bf16[512,1152]{1,0:T(8,128)(2,1)}), bf16[512,1152]{1,0:T(8,128)(2,1)}) %all-reduce.2.cloned.1.call-update) | async-done | bytes 1179664 | tf_op jit(solution)/shard_map/psum | solution.py:64
  80.5 3.1 convolution_convert_fusion.3
  83.6 13.5 %all_gather.7 = bf16[128,2048]{1,0:T(8,128)(2,1)S(1)} all-gather(bf16[128,512]{1,0:T(8,128)(2,1)S(1)} %convolution_convert_fusion.3), channel_id=1, replica_groups=mesh['section'=4,'dp'=8,'expert'=8] {'section'}, dimensions={1}, use_global_device_ids=true | all-gather | bytes 655360 | tf_op jit(solution)/shard_map/all_gather | solution.py:73
  97.4 7.1 %gather_fusion = bf16[1536,2048]{1,0:T(8,128)(2,1)} fusion(bf16[128,2048]{1,0:T(8,128)(2,1)S(1)} %fusion.21, s32[2048]{0:T(1024)S(1)} %pad_clamp_fusion), kind=kCustom, calls=%fused_computation | custom fusion | bytes 12589056 | tf_op jit(solution)/shard_map/gather | solution.py:87
  104.5 150.8 %all_to_all.10 = bf16[64,24,2048]{2,1,0:T(8,128)(2,1)S(1)} all-to-all(bf16[64,24,2048]{2,1,0:T(8,128)(2,1)} %bitcast.118), channel_id=1, replica_groups=mesh['section'=4,'dp'=8,'expert'=8] {'dp','expert'}, dimensions={0} | all-to-all | bytes 12582912 | tf_op jit(solution)/shard_map/all_to_all | solution.py:88
  255.3 2.7 copy-done.3
  258.0 3.8 fusion.14
  261.8 11.8 %convolution_convert_fusion = bf16[1536,2048]{1,0:T(8,128)(2,1)} fusion(bf16[1,352,2048]{2,1,0:T(8,128)(2,1)S(1)} %copy-done.7, bf16[1536,2048]{1,0:T(8,128)(2,1)} %bitcast.121, f32[1536,352]{0,1:T(8,128)} %fusion.14, bf16[1,2048,352]{1,2,0:T(8,128)(2,1)} %param.18), kind=kOutput, calls=%fused_computation.4 | convolution fusion | flops 4435574784 | bytes 17629184 | tf_op jit(solution)/shard_map/dot_general | solution.py:93
  273.6 7.5 %all-to-all-start.1 = ((bf16[64,24,2048]{2,1,0:T(8,128)(2,1)}), bf16[64,24,2048]{2,1,0:T(8,128)(2,1)}, u32[]{:S(2)}, u32[]{:S(2)}) async-start(bf16[64,24,2048]{2,1,0:T(8,128)(2,1)} %bitcast.119), calls=%async_computation.1 | async-start | bytes 12582912 | tf_op jit(solution)/shard_map/all_to_all | solution.py:94
  281.4 138.7 %all-to-all-done.1 = bf16[64,24,2048]{2,1,0:T(8,128)(2,1)} async-done(((bf16[64,24,2048]{2,1,0:T(8,128)(2,1)}), bf16[64,24,2048]{2,1,0:T(8,128)(2,1)}, u32[]{:S(2)}, u32[]{:S(2)}) %all-to-all-start.1) | async-done | bytes 6291488 | tf_op jit(solution)/shard_map/all_to_all | solution.py:94
  420.1 10.7 %gather_fusion.1 = bf16[768,2048]{1,0:T(8,128)(2,1)} fusion(bf16[1536,2048]{1,0:T(8,128)(2,1)} %bitcast.16, s32[1024]{0:T(1024)S(1)} %pad_clamp_fusion.1), kind=kCustom, calls=%fused_computation.1 | custom fusion | bytes 6294528 | tf_op jit(solution)/shard_map/gather | solution.py:101
  430.8 6.3 %reshape.176 = bf16[128,6,2048]{2,1,0:T(8,128)(2,1)} reshape(bf16[768,2048]{1,0:T(8,128)(2,1)} %gather_fusion.1) | data formatting | bytes 6291456 | tf_op jit(solution)/shard_map/reshape | solution.py:101
  437.1 15.9 %fusion.45 = (bf16[128,1,2048]{2,1,0:T(2,128)(2,1)S(1)}, bf16[128,1,2048]{2,1,0:T(2,128)(2,1)S(1)}, bf16[128,1,2048]{2,1,0:T(2,128)(2,1)S(1)}, bf16[128,1,2048]{...) fusion(bf16[128,6,2048]{2,1,0:T(8,128)(2,1)} %reshape.176), kind=kLoop, calls=%fused_computation.100 | loop fusion | bytes 6291456 | tf_op jit(solution)/shard_map/slice | solution.py:106
  453.1 4.2 fusion.23
  457.3 22.1 %reduce-scatter.2.cloned.1.call-done = bf16[128,512]{1,0:T(8,128)(2,1)} async-done(((bf16[128,2048]{1,0:T(8,128)(2,1)}), bf16[128,512]{1,0:T(8,128)(2,1)}) %reduce-scatter.2.cloned.1.call-update) | async-done | bytes 131088 | tf_op jit(solution)/shard_map/reduce_scatter | solution.py:109
  479.4 1.6 add_convert_fusion
  (53 shorter events, 5.3 us)
Async XLA Ops:
  7.4 3.9 copy-start
  7.4 3.9 copy-start.2
  7.4 3.4 copy-start.9
  7.4 70.7 %all-reduce.2.cloned.1.call-start = ((), (), s32[]{:S(2)}) async-start(), calls=%async_computation.3 | async-start | bytes 2359296 | tf_op jit(solution)/shard_map/psum | solution.py:64
  18.7 2.9 copy-start.8
  21.5 2.5 copy-start.4
  23.5 57.0 %all-gather.2.cloned.1.call-start = ((), (), s32[]{:S(2)}) async-start(), calls=%async_computation.4 | async-start | bytes 5308416 | tf_op jit(solution)/shard_map/all_gather | solution.py:71
  104.5 153.4 %copy-start.6 = (bf16[1,2048,352]{1,2,0:T(8,128)(2,1)S(1)}, bf16[1,2048,352]{1,2,0:T(8,128)(2,1)}, u32[]{:S(2)}) copy-start(bf16[1,2048,352]{1,2,0:T(8,128)(2,1)} %param.17) | copy-start | bytes 4325380
  255.3 2.7 copy-start.3
  258.0 3.8 copy-start.7
  273.6 7.8 %copy-start.5 = (f32[128,6]{0,1:T(8,128)S(1)}, f32[128,6]{0,1:T(8,128)}, u32[]{:S(2)}) copy-start(f32[128,6]{0,1:T(8,128)} %param.16) | copy-start | bytes 9220
  273.6 146.5 %all-to-all-start.1 = ((bf16[64,24,2048]{2,1,0:T(8,128)(2,1)}), bf16[64,24,2048]{2,1,0:T(8,128)(2,1)}, u32[]{:S(2)}, u32[]{:S(2)}) async-start(bf16[64,24,2048]{2,1,0:T(8,128)(2,1)} %bitcast.119), calls=%async_computation.1 | async-start | bytes 12582912 | tf_op jit(solution)/shard_map/all_to_all | solution.py:94
  281.1 198.3 %reduce-scatter.2.cloned.1.call-start = ((), (), s32[]{:S(2)}) async-start(), calls=%async_computation.5 | async-start | bytes 655360 | tf_op jit(solution)/shard_map/reduce_scatter | solution.py:109
  453.0 27.9 %copy-start.1 = (bf16[1152,864]{0,1:T(8,128)(2,1)S(1)}, bf16[1152,864]{0,1:T(8,128)(2,1)}, u32[]{:S(2)}) copy-start(bf16[1152,864]{0,1:T(8,128)(2,1)} %param.12) | copy-start | bytes 5971972
Sparse Core Ops, SparseCore 0:
  23.6 54.4 all-reduce.1
  457.4 21.9 reduce-scatter.1
Sparse Core Ops, SparseCore 1:
  25.8 38.5 all-gather.1
where the time goes:
time: 489 us; the launch traced here: 488 us
  waiting for transfers between devices  209 us (43%)
  blocking collectives  164 us (34%)
  local copies, waits for them, and re-layouts  47.7 us (10%)
  matrix products  30.9 us (6%)
  between operations  15.1 us (3%)
  other arithmetic  13.7 us (3%)
  starting transfers between devices  7.77 us (2%)
    all_to_all x1, blocking collectives, per_device(): lax.all_to_all(outgoing, ('dp', 'expert'), split_axis=0, concat_axis=0, t...  151 us
    all_to_all x1, waiting for transfers between devices, per_device(): lax.all_to_all(result.reshape(received.shape[:-1] + (w_down.shape[2],)),...  139 us
    psum x1, waiting for transfers between devices, per_device(): lax.psum(jnp.dot(attended, w_out, preferred_element_type=jnp.float32).ast...  47.7 us
    reduce_scatter x1, waiting for transfers between devices, per_device(): lax.psum_scatter(weighted.astype(jnp.bfloat16), 'section', scatter_dimens...  22.1 us
    slice x1, local copies, waits for them, and re-layouts, per_device(): picked[:, choice_index].astype(jnp.float32)  15.9 us
    all_gather x1, blocking collectives, per_device(): projected = lax.all_gather(proj_own, 'section', axis=1, tiled=True)  13.5 us
    dot_general x1, matrix products, per_device(): jnp.dot(hidden, w_down[0], preferred_element_type=jnp.float32)  11.8 us
    gather x1, local copies, waits for them, and re-layouts, per_device(): returned.reshape(expert_total * capacity, model_width)[target]  10.7 us
  transfers between devices with their start and end apart: 4, of which 3 were waited for; matrix products, arithmetic and copies ran while one was open for 2% of the time, Pallas kernels for 0%

commit v1 on v0

--- a/solution.py
+++ b/solution.py
@@ -61,8 +61,12 @@
     )
     attended = attended.reshape(patch_rows, local_heads * head_dim)
     merged_count = patch_rows // 4
-    summed = lax.psum(
-        jnp.dot(attended, w_out, preferred_element_type=jnp.float32).astype(jnp.bfloat16), "section"
+    summed = jnp.sum(
+        lax.all_gather(
+            jnp.dot(attended, w_out, preferred_element_type=jnp.float32).astype(jnp.bfloat16),
+            "section",
+        ),
+        axis=0,
     ).astype(jnp.float32)
     merged = (
         (patches.astype(jnp.float32) + summed).reshape(merged_count, 4 * width).astype(jnp.bfloat16)

time: 489 us -> 527 us (1.078)
  waiting for transfers between devices: 209 us -> 245 us
    all_gather x0 -> x1, waiting for transfers between devices: none -> 51 us  [per_device(): lax.all_gather(jnp.dot(attended, w_out, preferred_element_type=jnp.float3...]
    psum x1 -> x0, waiting for transfers between devices: 47.7 us -> none  [per_device(): lax.psum(jnp.dot(attended, w_out, preferred_element_type=jnp.float32).ast...]
    all_gather x1, waiting for transfers between devices: 0.03 us -> 31.4 us  [per_device(): lax.all_gather(w_proj, 'dp', axis=0, tiled=True)]
  transfers between devices with their start and end apart: 4 -> 4, of which waited for: 3 -> 4; matrix products, arithmetic and copies ran while one was open for 2% -> 2% of each run, Pallas kernels for 0% -> 0%
where the time goes in v1:
time: 527 us; the launch traced here: 526 us
  waiting for transfers between devices  245 us (46%)
  blocking collectives  164 us (31%)
  local copies, waits for them, and re-layouts  47.7 us (9%)
  matrix products  30.8 us (6%)
  other arithmetic  18 us (3%)
  between operations  13.3 us (3%)
  starting transfers between devices  7.55 us (1%)
    all_to_all x1, blocking collectives, per_device(): lax.all_to_all(outgoing, ('dp', 'expert'), split_axis=0, concat_axis=0, t...  151 us
    all_to_all x1, waiting for transfers between devices, per_device(): lax.all_to_all(result.reshape(received.shape[:-1] + (w_down.shape[2],)),...  139 us
    all_gather x1, waiting for transfers between devices, per_device(): lax.all_gather(jnp.dot(attended, w_out, preferred_element_type=jnp.float3...  51 us
    all_gather x1, waiting for transfers between devices, per_device(): lax.all_gather(w_proj, 'dp', axis=0, tiled=True)  31.4 us
    reduce_scatter x1, waiting for transfers between devices, per_device(): lax.psum_scatter(weighted.astype(jnp.bfloat16), 'section', scatter_dimens...  23.3 us
    slice x1, local copies, waits for them, and re-layouts, per_device(): picked[:, choice_index].astype(jnp.float32)  15.9 us
    all_gather x1, blocking collectives, per_device(): projected = lax.all_gather(proj_own, 'section', axis=1, tiled=True)  13.1 us
    dot_general x1, matrix products, per_device(): jnp.dot(hidden, w_down[0], preferred_element_type=jnp.float32)  11.8 us
  transfers between devices with their start and end apart: 4, of which 4 were waited for; matrix products, arithmetic and copies ran while one was open for 2% of the time, Pallas kernels for 0%

profile of v1, /device:TPU:8, one launch (start us, length us, event | category | flops | bytes accessed | tf_op | source)
XLA Modules:
  0.0 526.4 jit_solution(14866957658823767984)
XLA Ops:
  8.2 1.7 fusion.5
  10.5 2.4 convolution_convert_fusion.2
  12.9 4.9 fusion.46
  17.9 2.8 fusion.16
  20.7 1.9 convolution_convert_fusion.1
  23.8 1.8 reduce-window.19
  26.3 3.4 scatter_custom_fusion
  29.7 51.0 %all-gather.6.cloned.1.call-done = bf16[2048,1152]{1,0:T(8,128)(2,1)} async-done(((bf16[512,1152]{1,0:T(8,128)(2,1)}), bf16[2048,1152]{1,0:T(8,128)(2,1)}) %all-gather.6.cloned.1.call-update) | async-done | bytes 4718608 | tf_op jit(solution)/shard_map/all_gather | solution.py:65
  80.7 4.4 reduce_sum.73
  87.4 31.4 %all-gather.4.cloned.1.call-done = bf16[4608,512]{1,0:T(8,128)(2,1)} async-done(((bf16[576,512]{1,0:T(8,128)(2,1)}), bf16[4608,512]{1,0:T(8,128)(2,1)}) %all-gather.4.cloned.1.call-update) | async-done | bytes 4718608 | tf_op jit(solution)/shard_map/all_gather | solution.py:75
  118.9 3.1 convolution_convert_fusion.3
  122.0 13.1 %all_gather.15 = bf16[128,2048]{1,0:T(8,128)(2,1)S(1)} all-gather(bf16[128,512]{1,0:T(8,128)(2,1)S(1)} %convolution_convert_fusion.3), channel_id=1, replica_groups=mesh['section'=4,'dp'=8,'expert'=8] {'section'}, dimensions={1}, use_global_device_ids=true | all-gather | bytes 655360 | tf_op jit(solution)/shard_map/all_gather | solution.py:77
  135.4 7.1 %gather_fusion = bf16[1536,2048]{1,0:T(8,128)(2,1)} fusion(bf16[128,2048]{1,0:T(8,128)(2,1)S(1)} %fusion.21, s32[2048]{0:T(1024)S(1)} %pad_clamp_fusion), kind=kCustom, calls=%fused_computation | custom fusion | bytes 12589056 | tf_op jit(solution)/shard_map/gather | solution.py:91
  142.5 150.5 %all_to_all.10 = bf16[64,24,2048]{2,1,0:T(8,128)(2,1)S(1)} all-to-all(bf16[64,24,2048]{2,1,0:T(8,128)(2,1)} %bitcast.119), channel_id=1, replica_groups=mesh['section'=4,'dp'=8,'expert'=8] {'dp','expert'}, dimensions={0} | all-to-all | bytes 12582912 | tf_op jit(solution)/shard_map/all_to_all | solution.py:92
  293.0 2.7 copy-done.3
  295.7 3.8 fusion.14
  299.5 11.8 %convolution_convert_fusion = bf16[1536,2048]{1,0:T(8,128)(2,1)} fusion(bf16[1,352,2048]{2,1,0:T(8,128)(2,1)S(1)} %copy-done.7, bf16[1536,2048]{1,0:T(8,128)(2,1)} %bitcast.122, f32[1536,352]{0,1:T(8,128)} %fusion.14, bf16[1,2048,352]{1,2,0:T(8,128)(2,1)} %param.18), kind=kOutput, calls=%fused_computation.4 | convolution fusion | flops 4435574784 | bytes 17629184 | tf_op jit(solution)/shard_map/dot_general | solution.py:97
  311.3 7.5 %all-to-all-start.1 = ((bf16[64,24,2048]{2,1,0:T(8,128)(2,1)}), bf16[64,24,2048]{2,1,0:T(8,128)(2,1)}, u32[]{:S(2)}, u32[]{:S(2)}) async-start(bf16[64,24,2048]{2,1,0:T(8,128)(2,1)} %bitcast.120), calls=%async_computation.1 | async-start | bytes 12582912 | tf_op jit(solution)/shard_map/all_to_all | solution.py:98
  318.9 138.9 %all-to-all-done.1 = bf16[64,24,2048]{2,1,0:T(8,128)(2,1)} async-done(((bf16[64,24,2048]{2,1,0:T(8,128)(2,1)}), bf16[64,24,2048]{2,1,0:T(8,128)(2,1)}, u32[]{:S(2)}, u32[]{:S(2)}) %all-to-all-start.1) | async-done | bytes 6291488 | tf_op jit(solution)/shard_map/all_to_all | solution.py:98
  457.8 10.7 %gather_fusion.1 = bf16[768,2048]{1,0:T(8,128)(2,1)} fusion(bf16[1536,2048]{1,0:T(8,128)(2,1)} %bitcast.17, s32[1024]{0:T(1024)S(1)} %pad_clamp_fusion.1), kind=kCustom, calls=%fused_computation.1 | custom fusion | bytes 6294528 | tf_op jit(solution)/shard_map/gather | solution.py:105
  468.5 6.3 %reshape.176 = bf16[128,6,2048]{2,1,0:T(8,128)(2,1)} reshape(bf16[768,2048]{1,0:T(8,128)(2,1)} %gather_fusion.1) | data formatting | bytes 6291456 | tf_op jit(solution)/shard_map/reshape | solution.py:105
  474.8 15.9 %fusion.45 = (bf16[128,1,2048]{2,1,0:T(2,128)(2,1)S(1)}, bf16[128,1,2048]{2,1,0:T(2,128)(2,1)S(1)}, bf16[128,1,2048]{2,1,0:T(2,128)(2,1)S(1)}, bf16[128,1,2048]{...) fusion(bf16[128,6,2048]{2,1,0:T(8,128)(2,1)} %reshape.176), kind=kLoop, calls=%fused_computation.100 | loop fusion | bytes 6291456 | tf_op jit(solution)/shard_map/slice | solution.py:110
  490.8 4.2 fusion.23
  495.0 23.3 %reduce-scatter.2.cloned.1.call-done = bf16[128,512]{1,0:T(8,128)(2,1)} async-done(((bf16[128,2048]{1,0:T(8,128)(2,1)}), bf16[128,512]{1,0:T(8,128)(2,1)}) %reduce-scatter.2.cloned.1.call-update) | async-done | bytes 131088 | tf_op jit(solution)/shard_map/reduce_scatter | solution.py:113
  (54 shorter events, 8.4 us)
Async XLA Ops:
  6.5 3.9 copy-start
  6.5 3.9 copy-start.2
  6.5 3.4 copy-start.9
  6.5 74.2 %all-gather.6.cloned.1.call-start = ((), (), s32[]{:S(2)}) async-start(), calls=%async_computation.5 | async-start | bytes 5898240 | tf_op jit(solution)/shard_map/all_gather | solution.py:65
  17.9 2.9 copy-start.8
  20.7 2.7 copy-start.4
  22.6 96.3 %all-gather.4.cloned.1.call-start = ((), (), s32[]{:S(2)}) async-start(), calls=%async_computation.3 | async-start | bytes 5308416 | tf_op jit(solution)/shard_map/all_gather | solution.py:75
  142.5 153.2 %copy-start.6 = (bf16[1,2048,352]{1,2,0:T(8,128)(2,1)S(1)}, bf16[1,2048,352]{1,2,0:T(8,128)(2,1)}, u32[]{:S(2)}) copy-start(bf16[1,2048,352]{1,2,0:T(8,128)(2,1)} %param.17) | copy-start | bytes 4325380
  293.0 2.7 copy-start.3
  295.7 3.8 copy-start.7
  311.3 7.5 %copy-start.5 = (f32[128,6]{0,1:T(8,128)S(1)}, f32[128,6]{0,1:T(8,128)}, u32[]{:S(2)}) copy-start(f32[128,6]{0,1:T(8,128)} %param.16) | copy-start | bytes 9220
  311.3 146.5 %all-to-all-start.1 = ((bf16[64,24,2048]{2,1,0:T(8,128)(2,1)}), bf16[64,24,2048]{2,1,0:T(8,128)(2,1)}, u32[]{:S(2)}, u32[]{:S(2)}) async-start(bf16[64,24,2048]{2,1,0:T(8,128)(2,1)} %bitcast.120), calls=%async_computation.1 | async-start | bytes 12582912 | tf_op jit(solution)/shard_map/all_to_all | solution.py:98
  318.8 199.5 %reduce-scatter.2.cloned.1.call-start = ((), (), s32[]{:S(2)}) async-start(), calls=%async_computation.4 | async-start | bytes 655360 | tf_op jit(solution)/shard_map/reduce_scatter | solution.py:113
  490.7 29.2 %copy-start.1 = (bf16[1152,864]{0,1:T(8,128)(2,1)S(1)}, bf16[1152,864]{0,1:T(8,128)(2,1)}, u32[]{:S(2)}) copy-start(bf16[1152,864]{0,1:T(8,128)(2,1)} %param.12) | copy-start | bytes 5971972
Sparse Core Ops, SparseCore 0:
  22.7 57.9 all-gather.5
  82.6 36.2 all-gather.3
  495.1 23.1 reduce-scatter.1
